TPU v7x, 128 devices: a whole 4x4x4 slice. The times are simulated.
128 devices in a mesh: dp: 16 (over x, y), expert: 8 (over z, core).
Axes of the slice: x: 4, y: 4, z: 4, core: 2. Of those that a mesh axis runs over, the one named last changes fastest.
Arguments:
- tokens: bfloat16 [2048, 4096], P('dp', 'expert'), may hold values from -6 to 6
- output_gradient: bfloat16 [2048, 4096], P('dp', 'expert'), may hold values from -6 to 6
- routing: int32 [2048, 2], P('dp'), may hold values from 0 to 7, all different within a row; in each aligned block of 128 rows (0 to 127, 128 to 255, ...) at most 96 rows name the same one
- router_gate_values: float32 [2048, 2], P('dp'), may hold values from 0.1 to 0.9
- gate_weight: bfloat16 [8, 7168, 4096], P('expert', 'dp'), may hold values from -0.09375 to 0.09375
- up_weight: bfloat16 [8, 7168, 4096], P('expert', 'dp'), may hold values from -0.09375 to 0.09375
- down_weight: bfloat16 [8, 7168, 4096], P('expert', 'dp'), may hold values from -0.0625 to 0.0625
- adapter_lower_gate: bfloat16 [8, 16, 4096], P('expert'), may hold values from -0.09375 to 0.09375
- adapter_upper_gate: bfloat16 [8, 7168, 16], P('expert', 'dp'), may hold values from -0.375 to 0.375
- adapter_lower_up: bfloat16 [8, 16, 4096], P('expert'), may hold values from -0.09375 to 0.09375
- adapter_upper_up: bfloat16 [8, 7168, 16], P('expert', 'dp'), may hold values from -0.375 to 0.375
- adapter_lower_down: bfloat16 [8, 16, 7168], P('expert', None, 'dp'), may hold values from -0.0625 to 0.0625
- adapter_upper_down: bfloat16 [8, 4096, 16], P('expert'), may hold values from -0.375 to 0.375
Outputs:
- grad_x: bfloat16 [2048, 4096], P('dp', 'expert')
- grad_lora_a_gate: float32 [8, 16, 4096], P('expert')
- grad_lora_b_gate: float32 [8, 7168, 16], P('expert', 'dp')
- grad_lora_a_up: float32 [8, 16, 4096], P('expert')
- grad_lora_b_up: float32 [8, 7168, 16], P('expert', 'dp')
- grad_lora_a_down: float32 [8, 16, 7168], P('expert', None, 'dp')
- grad_lora_b_down: float32 [8, 4096, 16], P('expert')
Inputs may be any that keep to these rules, and one draw needn't show every extreme that they name: `routing`: each row names two different experts. In the rows of one dp shard (aligned blocks of 128 rows) no expert is named by more than 96 rows, and in some blocks one expert is named by exactly 96 rows.
All inputs are finite; a program needn't handle non-finite values.
Results may differ from a plain program's by a relative error of at most 0.015.
Values may be sent and summed in bfloat16 or wider, within the bound.
A program may use at most 256 MiB of HBM per device.

v0:
```python
import jax
import jax.numpy as jnp
from jax import lax
from jax.sharding import PartitionSpec as P

ADAPTER_SCALE = 2.0
NUM_CHUNKS = 2
PART_COLS = 128


def contract_pair(left, right, left_axis, right_axis):
    return lax.dot_general(
        left, right, (((left_axis,), (right_axis,)), ((), ())), preferred_element_type=jnp.float32
    )


def slot_numbers(route_rows, experts):
    picked = (route_rows[:, :, None] == jnp.arange(experts, dtype=jnp.int32)[None, None, :]).astype(
        jnp.int32
    )
    per_token = jnp.sum(picked, axis=1)
    earlier = jnp.cumsum(per_token, axis=0) - per_token
    return jnp.sum(earlier[:, None, :] * picked, axis=2)


def slot_sources(route_rows, positions, experts, capacity):
    tokens_here, choose = route_rows.shape
    target = (route_rows * capacity + positions).reshape(-1)
    owners = jnp.repeat(jnp.arange(tokens_here, dtype=jnp.int32), choose)
    member_ids = jnp.tile(jnp.arange(choose, dtype=jnp.int32), tokens_here)
    source = jnp.full((experts * capacity,), tokens_here, jnp.int32).at[target].set(owners)
    member = jnp.zeros((experts * capacity,), jnp.int32).at[target].set(member_ids)
    return (source, member)


def rows_backward_pass(input_rows, output_gradient_rows, params):
    (
        gate_weight,
        up_weight,
        down_weight,
        a_gate,
        gate_adapter_upper,
        a_up,
        up_adapter_upper,
        down_adapter_lower,
        b_down,
    ) = params
    gate_projected_lower = contract_pair(a_gate, input_rows, 1, 1).astype(jnp.bfloat16)
    up_projected_lower = contract_pair(a_up, input_rows, 1, 1).astype(jnp.bfloat16)
    gate_preactivation = contract_pair(
        gate_weight, input_rows, 1, 1
    ) + ADAPTER_SCALE * contract_pair(gate_adapter_upper, gate_projected_lower, 1, 0)
    up_preactivation = contract_pair(up_weight, input_rows, 1, 1) + ADAPTER_SCALE * contract_pair(
        up_adapter_upper, up_projected_lower, 1, 0
    )
    sigmoid_gate = jax.nn.sigmoid(gate_preactivation)
    silu_gate = gate_preactivation * sigmoid_gate
    hidden_units = (silu_gate * up_preactivation).astype(jnp.bfloat16)
    down_projected_lower = contract_pair(b_down, output_gradient_rows, 0, 1).astype(jnp.bfloat16)
    hidden_gradient = contract_pair(
        down_weight, output_gradient_rows, 1, 1
    ) + ADAPTER_SCALE * contract_pair(down_adapter_lower, down_projected_lower, 0, 0)
    gate_gradient = (
        hidden_gradient
        * up_preactivation
        * sigmoid_gate
        * (1.0 + gate_preactivation * (1.0 - sigmoid_gate))
    ).astype(jnp.bfloat16)
    up_gradient = (hidden_gradient * silu_gate).astype(jnp.bfloat16)
    gate_partial = contract_pair(gate_adapter_upper, gate_gradient, 0, 0).astype(jnp.bfloat16)
    up_partial = contract_pair(up_adapter_upper, up_gradient, 0, 0).astype(jnp.bfloat16)
    down_partial = contract_pair(down_adapter_lower, hidden_units, 1, 0).astype(jnp.bfloat16)
    paired_partials = jnp.concatenate([gate_partial, up_partial], 0)
    paired_factors = jnp.concatenate([a_gate, a_up], 0)
    gradient_rows_out = (
        contract_pair(gate_gradient, gate_weight, 0, 0)
        + contract_pair(up_gradient, up_weight, 0, 0)
        + ADAPTER_SCALE * contract_pair(paired_partials, paired_factors, 0, 0)
    )
    shared_slice = (
        ADAPTER_SCALE * contract_pair(gate_partial, input_rows, 1, 0),
        ADAPTER_SCALE * contract_pair(up_partial, input_rows, 1, 0),
        ADAPTER_SCALE * contract_pair(output_gradient_rows, down_partial, 0, 1),
    )
    owned_slice = (
        ADAPTER_SCALE * contract_pair(gate_gradient, gate_projected_lower, 1, 1),
        ADAPTER_SCALE * contract_pair(up_gradient, up_projected_lower, 1, 1),
        ADAPTER_SCALE * contract_pair(down_projected_lower, hidden_units, 1, 1),
    )
    return (gradient_rows_out, shared_slice, owned_slice)


def rows_backward_parts(input_rows, output_gradient_rows, params):
    (
        gate_weight,
        up_weight,
        down_weight,
        a_gate,
        gate_adapter_upper,
        a_up,
        up_adapter_upper,
        down_adapter_lower,
        b_down,
    ) = params
    gate_projected_lower = contract_pair(a_gate, input_rows, 1, 1).astype(jnp.bfloat16)
    up_projected_lower = contract_pair(a_up, input_rows, 1, 1).astype(jnp.bfloat16)
    gate_preactivation = contract_pair(
        gate_weight, input_rows, 1, 1
    ) + ADAPTER_SCALE * contract_pair(gate_adapter_upper, gate_projected_lower, 1, 0)
    up_preactivation = contract_pair(up_weight, input_rows, 1, 1) + ADAPTER_SCALE * contract_pair(
        up_adapter_upper, up_projected_lower, 1, 0
    )
    sigmoid_gate = jax.nn.sigmoid(gate_preactivation)
    silu_gate = gate_preactivation * sigmoid_gate
    hidden_units = (silu_gate * up_preactivation).astype(jnp.bfloat16)
    down_projected_lower = contract_pair(b_down, output_gradient_rows, 0, 1).astype(jnp.bfloat16)
    hidden_gradient = contract_pair(
        down_weight, output_gradient_rows, 1, 1
    ) + ADAPTER_SCALE * contract_pair(down_adapter_lower, down_projected_lower, 0, 0)
    gate_gradient = (
        hidden_gradient
        * up_preactivation
        * sigmoid_gate
        * (1.0 + gate_preactivation * (1.0 - sigmoid_gate))
    ).astype(jnp.bfloat16)
    up_gradient = (hidden_gradient * silu_gate).astype(jnp.bfloat16)
    gate_partial = contract_pair(gate_gradient, gate_adapter_upper, 0, 0).astype(jnp.bfloat16)
    up_partial = contract_pair(up_gradient, up_adapter_upper, 0, 0).astype(jnp.bfloat16)
    down_partial = contract_pair(hidden_units, down_adapter_lower, 0, 1).astype(jnp.bfloat16)
    paired_partials = jnp.concatenate([gate_partial, up_partial], 1)
    paired_factors = jnp.concatenate([a_gate, a_up], 0)
    gradient_rows_out = (
        contract_pair(gate_gradient, gate_weight, 0, 0)
        + contract_pair(up_gradient, up_weight, 0, 0)
        + ADAPTER_SCALE * contract_pair(paired_partials, paired_factors, 1, 0)
    )
    parts = jnp.concatenate([gate_partial, up_partial, down_partial], 1)
    owned_slice = (
        ADAPTER_SCALE * contract_pair(gate_gradient, gate_projected_lower, 1, 1),
        ADAPTER_SCALE * contract_pair(up_gradient, up_projected_lower, 1, 1),
        ADAPTER_SCALE * contract_pair(down_projected_lower, hidden_units, 1, 1),
    )
    return (gradient_rows_out, parts, owned_slice)


def local(
    tokens,
    output_gradient,
    routing,
    router_gate_values,
    gate_weight,
    up_weight,
    down_weight,
    adapter_lower_gate,
    adapter_upper_gate,
    adapter_lower_up,
    adapter_upper_up,
    adapter_lower_down,
    adapter_upper_down,
):
    experts = lax.axis_size("expert")
    shards = lax.axis_size("dp")
    tok_local, feat_local = tokens.shape
    choose = routing.shape[1]
    complete_width = feat_local * experts
    capacity = min(tok_local, 6 * tok_local // experts)
    adapter_rank = adapter_lower_gate.shape[1]
    chunks = NUM_CHUNKS
    piece = capacity // chunks
    params = (
        gate_weight[0],
        up_weight[0],
        down_weight[0],
        adapter_lower_gate[0],
        adapter_upper_gate[0],
        adapter_lower_up[0],
        adapter_upper_up[0],
        adapter_lower_down[0],
        adapter_upper_down[0],
    )
    positions = slot_numbers(routing, experts)
    zero_row = jnp.zeros((1, feat_local), jnp.bfloat16)
    source, member = slot_sources(routing, positions, experts, capacity)
    clamped = jnp.minimum(source, tok_local - 1)
    slot_gate = jnp.where(
        source < tok_local, router_gate_values.reshape(-1)[clamped * choose + member], 0.0
    )
    send_x = jnp.concatenate([tokens, zero_row], 0)[source].reshape(experts, capacity, feat_local)
    send_dy = (
        (
            slot_gate[:, None]
            * jnp.concatenate([output_gradient, zero_row], 0)[source].astype(jnp.float32)
        )
        .astype(jnp.bfloat16)
        .reshape(experts, capacity, feat_local)
    )
    send_both = jnp.concatenate([send_x, send_dy], axis=2)
    recv_both = lax.all_to_all(send_both, "expert", split_axis=0, concat_axis=2, tiled=True)[0]
    recv_both = recv_both.reshape(capacity, experts, 2, feat_local).transpose(0, 2, 1, 3)
    recv_both = recv_both.reshape(capacity, 2 * complete_width)
    rows_chunks = []
    part_chunks = []
    x_chunks = []
    dy_chunks = []
    owned_total = None
    for c in range(chunks):
        part = recv_both[c * piece : (c + 1) * piece]
        gathered = lax.all_gather(part, "dp", axis=0, tiled=True)
        x_rows = gathered[:, :complete_width]
        dy_rows = gathered[:, complete_width:]
        rows_out, parts, owned_slice = rows_backward_parts(x_rows, dy_rows, params)
        if c == 0:
            owned_total = owned_slice
        else:
            owned_total = jax.tree.map(jnp.add, owned_total, owned_slice)
        rows_chunks.append(rows_out.astype(jnp.bfloat16).reshape(shards, piece, complete_width))
        part_chunks.append(parts.reshape(shards, piece, 3 * adapter_rank))
        x_chunks.append(x_rows.reshape(shards, piece, complete_width))
        dy_chunks.append(dy_rows.reshape(shards, piece, complete_width))
    rows_all = jnp.concatenate(rows_chunks, 1)
    parts_all = jnp.concatenate(part_chunks, 1)
    parts_all = jnp.pad(parts_all, ((0, 0), (0, 0), (0, PART_COLS - 3 * adapter_rank)))
    packed = jnp.concatenate([rows_all, parts_all], 2)
    summed_packed = lax.psum_scatter(packed, "dp", scatter_dimension=0, tiled=True)[0]
    summed = summed_packed[:, :complete_width]
    parts_mine = summed_packed[:, complete_width : complete_width + 3 * adapter_rank]
    parts_sum = lax.all_gather(parts_mine, "dp", axis=0, tiled=True)
    parts_sum = parts_sum.reshape(shards, capacity, 3 * adapter_rank)
    x_all = jnp.concatenate(x_chunks, 1).reshape(shards * capacity, complete_width)
    dy_all = jnp.concatenate(dy_chunks, 1).reshape(shards * capacity, complete_width)
    parts_sum = parts_sum.reshape(shards * capacity, 3 * adapter_rank)
    grad_a_gate = ADAPTER_SCALE * contract_pair(parts_sum[:, :adapter_rank], x_all, 0, 0)
    grad_a_up = ADAPTER_SCALE * contract_pair(
        parts_sum[:, adapter_rank : 2 * adapter_rank], x_all, 0, 0
    )
    grad_b_down = ADAPTER_SCALE * contract_pair(dy_all, parts_sum[:, 2 * adapter_rank :], 0, 0)
    returned_rows = lax.all_to_all(
        summed.reshape(capacity, experts, feat_local),
        "expert",
        split_axis=1,
        concat_axis=1,
        tiled=True,
    ).astype(jnp.float32)
    lookup = positions * experts + routing
    grad_x = jnp.sum(returned_rows.reshape(capacity * experts, feat_local)[lookup], axis=1).astype(
        jnp.bfloat16
    )
    return (
        grad_x,
        grad_a_gate[None],
        owned_total[0][None],
        grad_a_up[None],
        owned_total[1][None],
        owned_total[2][None],
        grad_b_down[None],
    )


def solution(mesh):
    return jax.shard_map(
        local,
        mesh=mesh,
        in_specs=(
            P("dp", "expert"),
            P("dp", "expert"),
            P("dp", None),
            P("dp", None),
            P("expert", "dp", None),
            P("expert", "dp", None),
            P("expert", "dp", None),
            P("expert", None, None),
            P("expert", "dp", None),
            P("expert", None, None),
            P("expert", "dp", None),
            P("expert", None, "dp"),
            P("expert", None, None),
        ),
        out_specs=(
            P("dp", "expert"),
            P("expert", None, None),
            P("expert", "dp", None),
            P("expert", None, None),
            P("expert", "dp", None),
            P("expert", None, "dp"),
            P("expert", None, None),
        ),
        check_vma=False,
    )
```

profile of v0, /device:TPU:1, one launch (start us, length us, event | category | flops | bytes accessed | tf_op | source)
XLA Modules:
  0.0 469.6 jit_solution(13800577406468424391)
XLA Ops:
  11.3 1.4 scatter_custom_fusion.1
  12.7 1.4 scatter_custom_fusion
  14.1 5.0 %gather_fusion.1 = f32[768]{0:T(1024)S(1)} fusion(f32[256]{0:T(256)S(1)} %reshape.120, s32[1024]{0:T(1024)S(1)} %get-tuple-element.23), kind=kCustom, calls=%fused_computation.1 | custom fusion | bytes 9216 | tf_op jit(solution)/shard_map/gather | solution.py:186
  19.2 2.7 gather_fusion.2
  21.9 2.7 gather_fusion
  25.1 27.4 %all_to_all.20 = bf16[8,96,1024]{2,1,0:T(8,128)(2,1)S(1)} all-to-all(bf16[8,96,1024]{2,1,0:T(8,128)(2,1)S(1)} %pad_maximum_fusion.3), channel_id=1, replica_groups=mesh['dp'=16,'expert'=8] {'expert'}, dimensions={0} | all-to-all | bytes 3145728 | tf_op jit(solution)/shard_map/all_to_all | solution.py:198
  53.6 1.7 copy.99
  55.4 1.3 fusion.94
  56.9 1.4 copy.94
  58.4 1.3 copy.95
  60.3 87.8 %all-gather.4.cloned.1.call-done = bf16[768,8192]{1,0:T(8,128)(2,1)} async-done(((bf16[48,8192]{1,0:T(8,128)(2,1)}), bf16[768,8192]{1,0:T(8,128)(2,1)}) %all-gather.4.cloned.1.call-update) | async-done | bytes 12582928 | tf_op jit(solution)/shard_map/all_gather | solution.py:208
  148.2 4.7 convolution_convert_fusion.11
  152.9 6.0 %fusion.21 = f32[768,448]{0,1:T(8,128)S(1)} fusion(bf16[1,448,4096]{2,1,0:T(8,128)(2,1)S(1)} %copy-done.29, bf16[768,8192]{1,0:T(8,128)(2,1)} %all-gather.4.cloned.1.call-done), kind=kOutput, calls=%fused_computation.35 | convolution fusion | flops 2818572288 | bytes 11337728 | tf_op jit(solution)/shard_map/dot_general | solution.py:12
  159.4 1.7 convolution_convert_fusion.10
  161.7 3.1 fusion.17
  165.2 1.7 convolution_convert_fusion.9
  167.3 3.3 fusion.9
  170.6 1.9 multiply_convert_fusion.5
  172.9 6.4 %fusion.15 = f32[768,4096]{1,0:T(8,128)} fusion(bf16[448,768]{1,0:T(8,128)(2,1)S(1)} %get-tuple-element.13, bf16[1,448,4096]{2,1,0:T(8,128)(2,1)S(1)} %copy-done.3), kind=kOutput, calls=%fused_computation.29 | convolution fusion | flops 2818572288 | bytes 16941056 | tf_op jit(solution)/shard_map/dot_general | solution.py:12
  179.3 6.3 %fusion.7 = f32[768,4096]{1,0:T(8,128)} fusion(bf16[448,768]{1,0:T(8,128)(2,1)S(1)} %get-tuple-element.11, bf16[1,448,4096]{2,1,0:T(8,128)(2,1)S(1)} %copy-done.5), kind=kOutput, calls=%fused_computation.21 | convolution fusion | flops 2818572288 | bytes 16941056 | tf_op jit(solution)/shard_map/dot_general | solution.py:12
  185.6 54.4 %all-gather.6.cloned.1.call-done = bf16[768,8192]{1,0:T(8,128)(2,1)} async-done(((bf16[48,8192]{1,0:T(8,128)(2,1)}), bf16[768,8192]{1,0:T(8,128)(2,1)}) %all-gather.6.cloned.1.call-update) | async-done | bytes 12582928 | tf_op jit(solution)/shard_map/all_gather | solution.py:208
  240.0 4.7 convolution_convert_fusion.8
  244.7 6.0 %fusion.19 = f32[768,448]{0,1:T(8,128)S(1)} fusion(bf16[1,448,4096]{2,1,0:T(8,128)(2,1)S(1)} %copy-done.30, bf16[768,8192]{1,0:T(8,128)(2,1)} %all-gather.6.cloned.1.call-done), kind=kOutput, calls=%fused_computation.33 | convolution fusion | flops 2818572288 | bytes 11337728 | tf_op jit(solution)/shard_map/dot_general | solution.py:12
  251.1 1.7 convolution_convert_fusion.7
  253.1 3.1 fusion.13
  256.6 1.7 convolution_convert_fusion.6
  258.7 3.5 fusion.5
  263.3 6.3 %fusion.11 = f32[768,4096]{1,0:T(8,128)} fusion(bf16[448,768]{1,0:T(8,128)(2,1)S(1)} %get-tuple-element.16, bf16[1,448,4096]{2,1,0:T(8,128)(2,1)S(1)} %copy-done.4), kind=kOutput, calls=%fused_computation.25 | convolution fusion | flops 2818572288 | bytes 16941056 | tf_op jit(solution)/shard_map/dot_general | solution.py:12
  269.9 6.3 %fusion.3 = f32[768,4096]{1,0:T(8,128)} fusion(bf16[448,768]{1,0:T(8,128)(2,1)S(1)} %get-tuple-element.14, bf16[1,448,4096]{2,1,0:T(8,128)(2,1)S(1)} %copy-done.6), kind=kOutput, calls=%fused_computation.17 | convolution fusion | flops 2818572288 | bytes 16941056 | tf_op jit(solution)/shard_map/dot_general | solution.py:12
  276.6 1.3 convolution_convert_fusion.1
  278.3 9.3 %add_convert_fusion.1 = bf16[768,4096]{1,0:T(8,128)(2,1)S(1)} fusion(f32[768,4096]{1,0:T(8,128)} %fusion.7, f32[768,4096]{1,0:T(8,128)} %fusion.15, bf16[16,4096]{1,0:T(8,128)(2,1)S(1)} %bitcast.196, bf16[16,4096]{1,0:T(8,128)(2,1)S(1)} %bitcast.198, bf16[768,16]{0,1:T(8,128)(2,1)} %copy-done.13, bf16[768,16]{0,1:T(8,128)(2,1)} %copy-done.12), kind=kOutput, calls=%fused_computation.10 | convolution fusion | flops 214532096 | bytes 31768576 | tf_op jit(solution)/shard_map/dot_general | solution.py:12
  287.5 12.0 %add_convert_fusion = bf16[768,4096]{1,0:T(8,128)(2,1)} fusion(f32[768,4096]{1,0:T(8,128)} %fusion.3, f32[768,4096]{1,0:T(8,128)} %fusion.11, bf16[16,4096]{1,0:T(8,128)(2,1)S(1)} %bitcast.197, bf16[16,4096]{1,0:T(8,128)(2,1)S(1)} %bitcast.199, bf16[768,16]{0,1:T(8,128)(2,1)S(1)} %convolution_convert_fusion.2, bf16[768,16]{0,1:T(8,128)(2,1)S(1)} %convolution_convert_fusion.3), kind=kOutput, calls=%fused_computation.9 | convolution fusion | flops 214532096 | bytes 31768576 | tf_op jit(solution)/shard_map/dot_general | solution.py:12
  299.5 10.4 %pad_maximum_fusion = bf16[16,96,4224]{2,1,0:T(8,128)(2,1)} fusion(bf16[16,96,128]{2,1,0:T(8,128)(2,1)S(1)} %fusion.46, bf16[16,48,4096]{2,1,0:T(8,128)(2,1)} %bitcast.176, bf16[16,48,4096]{2,1,0:T(8,128)(2,1)S(1)} %bitcast.172), kind=kLoop, calls=%fused_computation.6 | loop fusion | flops 38928384 | bytes 25952256 | tf_op jit(solution)/shard_map/concatenate | solution.py:223
  310.7 1.4 fusion.97
  312.1 2.1 fusion.39
  316.6 5.9 %fusion.93 = (bf16[768,4096]{1,0:T(8,128)(2,1)S(1)}, bf16[768,4096]{1,0:T(8,128)(2,1)S(1)}) fusion(bf16[768,8192]{1,0:T(8,128)(2,1)} %all-gather.6.cloned.1.call-done), kind=kLoop, calls=%fused_computation.158 | loop fusion | bytes 25165824 | tf_op jit(solution)/shard_map/slice | solution.py:210
  322.5 5.7 %fusion.92 = (bf16[768,4096]{1,0:T(8,128)(2,1)S(1)}, bf16[768,4096]{1,0:T(8,128)(2,1)S(1)}) fusion(bf16[768,8192]{1,0:T(8,128)(2,1)} %all-gather.4.cloned.1.call-done), kind=kLoop, calls=%fused_computation.157 | loop fusion | bytes 25165824 | tf_op jit(solution)/shard_map/slice | solution.py:210
  328.2 8.7 %pad_maximum_fusion.2 = bf16[16,96,4096]{2,1,0:T(8,128)(2,1)} fusion(bf16[16,48,4096]{2,1,0:T(8,128)(2,1)S(1)} %bitcast.174, bf16[16,48,4096]{2,1,0:T(8,128)(2,1)S(1)} %bitcast.177), kind=kLoop, calls=%fused_computation.8 | loop fusion | flops 25165824 | bytes 25165824 | tf_op jit(solution)/shard_map/concatenate | solution.py:230
  336.9 8.6 %pad_maximum_fusion.1 = bf16[16,96,4096]{2,1,0:T(8,128)(2,1)} fusion(bf16[16,48,4096]{2,1,0:T(8,128)(2,1)S(1)} %bitcast.173, bf16[16,48,4096]{2,1,0:T(8,128)(2,1)S(1)} %bitcast.175), kind=kLoop, calls=%fused_computation.7 | loop fusion | flops 25165824 | bytes 25165824 | tf_op jit(solution)/shard_map/concatenate | solution.py:229
  345.5 60.0 %reduce-scatter.4.cloned.1.call-done = bf16[1,96,4224]{2,1,0:T(8,128)(2,1)} async-done(((bf16[16,96,4224]{2,1,0:T(8,128)(2,1)}), bf16[1,96,4224]{2,1,0:T(8,128)(2,1)}) %reduce-scatter.4.cloned.1.call-update) | async-done | bytes 811024
  406.3 1.2 slice.66
  407.5 16.7 %all-gather = bf16[16,96,48]{1,2,0:T(8,128)(2,1)S(1)} all-gather(bf16[1,96,48]{1,2,0:T(8,128)(2,1)S(1)} %copy.88), channel_id=1, replica_groups=mesh['dp'=16,'expert'=8] {'dp'}, dimensions={0}, use_global_device_ids=true | all-gather | bytes 156672 | tf_op jit(solution)/shard_map/all_gather | solution.py:227
  424.5 7.2 %fusion.1 = f32[1,16,4096]{2,1,0:T(8,128)} fusion(bf16[1536,4096]{1,0:T(8,128)(2,1)} %bitcast.169, bf16[1536,48]{0,1:T(8,128)(2,1)S(1)} %reshape.191), kind=kOutput, calls=%fused_computation.14 | convolution fusion | flops 201392128 | bytes 12894208 | tf_op jit(solution)/shard_map/dot_general | solution.py:12
  432.7 2.4 fusion.2
  436.2 11.4 %all-to-all-start.1 = ((bf16[96,8,512]{2,0,1:T(8,128)(2,1)}), bf16[96,8,512]{2,0,1:T(8,128)(2,1)S(1)}, u32[]{:S(2)}, u32[]{:S(2)}) async-start(bf16[96,8,512]{2,0,1:T(8,128)(2,1)} %bitcast.166), calls=%async_computation.1 | async-start | bytes 1572864 | tf_op jit(solution)/shard_map/all_to_all | solution.py:237
  447.6 7.0 %fusion = f32[1,4096,16]{1,2,0:T(8,128)} fusion(bf16[1536,4096]{1,0:T(8,128)(2,1)} %bitcast.171, bf16[1536,48]{0,1:T(8,128)(2,1)S(1)} %reshape.191), kind=kOutput, calls=%fused_computation.12 | convolution fusion | flops 201392128 | bytes 12894208 | tf_op jit(solution)/shard_map/dot_general | solution.py:12
  454.6 5.3 %all-to-all-done.1 = bf16[96,8,512]{2,0,1:T(8,128)(2,1)S(1)} async-done(((bf16[96,8,512]{2,0,1:T(8,128)(2,1)}), bf16[96,8,512]{2,0,1:T(8,128)(2,1)S(1)}, u32[]{:S(2)}, u32[]{:S(2)}) %all-to-all-start.1) | async-done | bytes 786464 | tf_op jit(solution)/shard_map/all_to_all | solution.py:237
  461.6 1.3 reduce_sum.29
  (139 shorter events, 20.4 us)
Async XLA Ops:
  7.2 141.0 %copy-start = (bf16[1,4096,16]{1,2,0:T(8,128)(2,1)S(1)}, bf16[1,4096,16]{1,2,0:T(8,128)(2,1)}, u32[]{:S(2)}) copy-start(bf16[1,4096,16]{1,2,0:T(8,128)(2,1)} %param.25) | copy-start | bytes 393220
  7.2 12.0 %copy-start.14 = (bf16[128,512]{1,0:T(8,128)(2,1)S(1)}, bf16[128,512]{1,0:T(8,128)(2,1)}, u32[]{:S(2)}) copy-start(bf16[128,512]{1,0:T(8,128)(2,1)} %param.13) | copy-start | bytes 393220
  7.2 12.0 %copy-start.15 = (bf16[128,512]{1,0:T(8,128)(2,1)S(1)}, bf16[128,512]{1,0:T(8,128)(2,1)}, u32[]{:S(2)}) copy-start(bf16[128,512]{1,0:T(8,128)(2,1)} %param.14) | copy-start | bytes 393220
  7.2 141.0 %all-gather.4.cloned.1.call-start = ((), (), s32[]{:S(2)}) async-start(), calls=%async_computation.3 | async-start | bytes 13369344 | tf_op jit(solution)/shard_map/all_gather | solution.py:208
  58.3 181.7 %all-gather.6.cloned.1.call-start = ((), (), s32[]{:S(2)}) async-start(), calls=%async_computation.4 | async-start | bytes 13369344 | tf_op jit(solution)/shard_map/all_gather | solution.py:208
  59.8 345.7 %reduce-scatter.4.cloned.1.call-start = ((), (), s32[]{:S(2)}) async-start(), calls=%async_computation.5 | async-start | bytes 13787136
  148.2 4.7 copy-start.29
  148.2 11.1 %slice-start = ((s8[12582912]{0:T(1024)(128)(4,1)}), s8[4194304]{0:T(1024)(128)(4,1)S(1)}, s32[]{:S(2)}) async-start(s8[12582912]{0:T(1024)(128)(4,1)} %bitcast.179), calls=%async_computation.6 | async-start | bytes 8388608
  152.8 6.0 %copy-start.18 = (bf16[768,16]{0,1:T(8,128)(2,1)}, bf16[768,16]{0,1:T(8,128)(2,1)S(1)}, u32[]{:S(2)}) copy-start(bf16[768,16]{0,1:T(8,128)(2,1)S(1)} %convolution_convert_fusion.11) | copy-start | bytes 73732
  152.8 6.0 %copy-start.11 = (bf16[1,16,448]{2,1,0:T(8,128)(2,1)S(1)}, bf16[1,16,448]{2,1,0:T(8,128)(2,1)}, u32[]{:S(2)}) copy-start(bf16[1,16,448]{2,1,0:T(8,128)(2,1)} %param.24) | copy-start | bytes 43012
  152.9 6.4 %slice-start.1 = ((s8[12582912]{0:T(1024)(128)(4,1)}), s8[4194304]{0:T(1024)(128)(4,1)S(1)}, s32[]{:S(2)}) async-start(s8[12582912]{0:T(1024)(128)(4,1)} %bitcast.179), calls=%async_computation.7 | async-start | bytes 8388608
  152.9 6.4 %slice-start.2 = ((s8[12582912]{0:T(1024)(128)(4,1)}), s8[4194304]{0:T(1024)(128)(4,1)S(1)}, s32[]{:S(2)}) async-start(s8[12582912]{0:T(1024)(128)(4,1)} %bitcast.179), calls=%async_computation.8 | async-start | bytes 8388608
  152.9 6.4 %copy-start.8 = (bf16[1,16,4096]{2,1,0:T(8,128)(2,1)S(1)}, bf16[1,16,4096]{2,1,0:T(8,128)(2,1)}, u32[]{:S(2)}) copy-start(bf16[1,16,4096]{2,1,0:T(8,128)(2,1)} %param.22) | copy-start | bytes 393220
  159.3 2.4 copy-start.3
  161.7 3.1 copy-start.16
  161.7 3.1 copy-start.10
  161.7 3.5 copy-start.9
  165.2 2.1 copy-start.5
  167.3 3.3 copy-start.25
  167.3 3.3 copy-start.24
  172.7 105.2 %copy-start.12 = (bf16[768,16]{0,1:T(8,128)(2,1)}, bf16[768,16]{0,1:T(8,128)(2,1)S(1)}, u32[]{:S(2)}) copy-start(bf16[768,16]{0,1:T(8,128)(2,1)S(1)} %convolution_convert_fusion.5) | copy-start | bytes 73732
  172.9 105.0 %copy-start.13 = (bf16[768,16]{0,1:T(8,128)(2,1)}, bf16[768,16]{0,1:T(8,128)(2,1)S(1)}, u32[]{:S(2)}) copy-start(bf16[768,16]{0,1:T(8,128)(2,1)S(1)} %convolution_convert_fusion.4) | copy-start | bytes 73732
  240.0 4.7 copy-start.30
  240.0 11.1 %slice-start.3 = ((s8[12582912]{0:T(1024)(128)(4,1)}), s8[4194304]{0:T(1024)(128)(4,1)S(1)}, s32[]{:S(2)}) async-start(s8[12582912]{0:T(1024)(128)(4,1)} %bitcast.181), calls=%async_computation.9 | async-start | bytes 8388608
  244.6 6.0 %copy-start.22 = (bf16[768,16]{0,1:T(8,128)(2,1)}, bf16[768,16]{0,1:T(8,128)(2,1)S(1)}, u32[]{:S(2)}) copy-start(bf16[768,16]{0,1:T(8,128)(2,1)S(1)} %convolution_convert_fusion.8) | copy-start | bytes 73732
  244.6 6.4 %slice-start.4 = ((s8[12582912]{0:T(1024)(128)(4,1)}), s8[4194304]{0:T(1024)(128)(4,1)S(1)}, s32[]{:S(2)}) async-start(s8[12582912]{0:T(1024)(128)(4,1)} %bitcast.181), calls=%async_computation.10 | async-start | bytes 8388608
  244.7 6.4 %slice-start.5 = ((s8[12582912]{0:T(1024)(128)(4,1)}), s8[4194304]{0:T(1024)(128)(4,1)S(1)}, s32[]{:S(2)}) async-start(s8[12582912]{0:T(1024)(128)(4,1)} %bitcast.181), calls=%async_computation.11 | async-start | bytes 8388608
  251.1 2.0 copy-start.4
  253.1 3.1 copy-start.20
  256.6 2.0 copy-start.6
  258.7 3.5 copy-start.27
  263.1 13.1 %copy-start.7 = (bf16[448,768]{1,0:T(8,128)(2,1)}, bf16[448,768]{1,0:T(8,128)(2,1)S(1)}, u32[]{:S(2)}) copy-start(bf16[448,768]{1,0:T(8,128)(2,1)S(1)} %get-tuple-element.15) | copy-start | bytes 2064388
  309.9 0.7 copy-start.19
  309.9 2.1 copy-start.23
  309.9 4.2 copy-start.26
  309.9 4.5 copy-start.28
  309.9 5.4 %copy-start.17 = (bf16[768,16]{0,1:T(8,128)(2,1)S(1)}, bf16[768,16]{0,1:T(8,128)(2,1)}, u32[]{:S(2)}) copy-start(bf16[768,16]{0,1:T(8,128)(2,1)} %copy-done.16) | copy-start | bytes 73732
  310.0 5.7 %copy-start.21 = (bf16[768,16]{0,1:T(8,128)(2,1)S(1)}, bf16[768,16]{0,1:T(8,128)(2,1)}, u32[]{:S(2)}) copy-start(bf16[768,16]{0,1:T(8,128)(2,1)} %copy-done.20) | copy-start | bytes 73732
  424.5 8.3 %copy-start.2 = (bf16[16,96,4096]{2,1,0:T(8,128)(2,1)S(1)}, bf16[16,96,4096]{2,1,0:T(8,128)(2,1)}, u32[]{:S(2)}) copy-start(bf16[16,96,4096]{2,1,0:T(8,128)(2,1)} %pad_maximum_fusion.1) | copy-start | bytes 37748740
  436.2 23.7 %all-to-all-start.1 = ((bf16[96,8,512]{2,0,1:T(8,128)(2,1)}), bf16[96,8,512]{2,0,1:T(8,128)(2,1)S(1)}, u32[]{:S(2)}, u32[]{:S(2)}) async-start(bf16[96,8,512]{2,0,1:T(8,128)(2,1)} %bitcast.166), calls=%async_computation.1 | async-start | bytes 1572864 | tf_op jit(solution)/shard_map/all_to_all | solution.py:237
  459.9 3.1 copy-start.1
Sparse Core Ops, SparseCore 0:
  58.4 89.7 all-gather.3
  150.3 89.5 all-gather.5
  310.1 95.3 reduce-scatter.3
where the time goes:
time: 477 us; the launch traced here: 470 us
  waiting for transfers between devices  207 us (43%)
  matrix products  117 us (25%)
  blocking collectives  44.1 us (9%)
  local copies, waits for them, and re-layouts  42.5 us (9%)
  other arithmetic  32 us (7%)
  between operations  14.6 us (3%)
  starting transfers between devices  12 us (3%)
    all_gather x2, waiting for transfers between devices, local(): gathered = lax.all_gather(part, 'dp', axis=0, tiled=True)  142 us
    dot_general x39, matrix products, contract_pair(): lax.dot_general(left, right, (((left_axis,), (right_axis,)), ((), ())), p...  117 us
    unnamed x4, waiting for transfers between devices  60 us
    all_to_all x1, blocking collectives, local(): lax.all_to_all(send_both, 'expert', split_axis=0, concat_axis=2, tiled=True)  27.4 us
    all_gather x1, blocking collectives, local(): parts_sum = lax.all_gather(parts_mine, 'dp', axis=0, tiled=True)  16.7 us
    slice x2, local copies, waits for them, and re-layouts, local(): dy_rows = gathered[:, complete_width:]  11.6 us
    all_to_all x1, starting transfers between devices, local(): lax.all_to_all(summed.reshape(capacity, experts, feat_local), 'expert', s...  11.4 us
    concatenate x1, other arithmetic, local(): packed = jnp.concatenate([rows_all, parts_all], 2)  10.4 us
  transfers between devices with their start and end apart: 4, of which 4 were waited for; matrix products, arithmetic and copies ran while one was open for 17% of the time, Pallas kernels for 0%

commit v1 on v0

--- a/solution.py
+++ b/solution.py
@@ -205,7 +205,9 @@
     owned_total = None
     for c in range(chunks):
         part = recv_both[c * piece : (c + 1) * piece]
-        gathered = lax.all_gather(part, "dp", axis=0, tiled=True)
+        gathered = jnp.concatenate(
+            lax.all_to_all(jnp.stack([part] * lax.axis_size("dp")), "dp", 0, 0), axis=0
+        )
         x_rows = gathered[:, :complete_width]
         dy_rows = gathered[:, complete_width:]
         rows_out, parts, owned_slice = rows_backward_parts(x_rows, dy_rows, params)

time: 477 us -> 818 us (1.71)
  waiting for transfers between devices: 207 us -> 494 us
  matrix products: 117 us -> 139 us
  starting transfers between devices: 12 us -> 30.9 us
  local copies, waits for them, and re-layouts: 42.5 us -> 52.7 us
    all_to_all x0 -> x2, waiting for transfers between devices: none -> 417 us  [local(): lax.all_to_all(jnp.stack([part] * lax.axis_size('dp')), 'dp', 0, 0)]
    all_gather x2 -> x0, waiting for transfers between devices: 142 us -> none  [local(): gathered = lax.all_gather(part, 'dp', axis=0, tiled=True)]
    dot_general x39, matrix products: 117 us -> 139 us  [contract_pair(): lax.dot_general(left, right, (((left_axis,), (right_axis,)), ((), ())), p...]
    all_to_all x0 -> x2, starting transfers between devices: none -> 19.2 us  [local(): lax.all_to_all(jnp.stack([part] * lax.axis_size('dp')), 'dp', 0, 0)]
    another operation x0 -> x2, local copies, waits for them, and re-layouts: none -> 12.2 us  [local(): jnp.stack([part] * lax.axis_size('dp'))]
    unnamed x4 -> x2, waiting for transfers between devices: 60 us -> 72 us
  transfers between devices with their start and end apart: 4 -> 4, of which waited for: 4 -> 4; matrix products, arithmetic and copies ran while one was open for 17% -> 6% of each run, Pallas kernels for 0% -> 0%
where the time goes in v1:
time: 818 us; the launch traced here: 808 us
  waiting for transfers between devices  494 us (60%)
  matrix products  139 us (17%)
  local copies, waits for them, and re-layouts  52.7 us (6%)
  blocking collectives  43.9 us (5%)
  other arithmetic  32.1 us (4%)
  starting transfers between devices  30.9 us (4%)
  between operations  15.1 us (2%)
    all_to_all x2, waiting for transfers between devices, local(): lax.all_to_all(jnp.stack([part] * lax.axis_size('dp')), 'dp', 0, 0)  417 us
    dot_general x39, matrix products, contract_pair(): lax.dot_general(left, right, (((left_axis,), (right_axis,)), ((), ())), p...  139 us
    unnamed x2, waiting for transfers between devices  72 us
    all_to_all x1, blocking collectives, local(): lax.all_to_all(send_both, 'expert', split_axis=0, concat_axis=2, tiled=True)  27.4 us
    all_to_all x2, starting transfers between devices, local(): lax.all_to_all(jnp.stack([part] * lax.axis_size('dp')), 'dp', 0, 0)  19.2 us
    all_gather x1, blocking collectives, local(): parts_sum = lax.all_gather(parts_mine, 'dp', axis=0, tiled=True)  16.5 us
  transfers between devices with their start and end apart: 4, of which 4 were waited for; matrix products, arithmetic and copies ran while one was open for 6% of the time, Pallas kernels for 0%

profile of v1, /device:TPU:1, one launch (start us, length us, event | category | flops | bytes accessed | tf_op | source)
XLA Modules:
  0.0 808.1 jit_solution(10096176300103558296)
XLA Ops:
  11.1 1.4 scatter_custom_fusion.1
  12.6 1.4 scatter_custom_fusion
  14.0 5.0 gather_fusion.1
  20.9 2.7 gather_fusion.2
  23.6 2.7 gather_fusion
  26.7 27.4 %all_to_all.30 = bf16[8,96,1024]{2,1,0:T(8,128)(2,1)S(1)} all-to-all(bf16[8,96,1024]{2,1,0:T(8,128)(2,1)S(1)} %pad_maximum_fusion.3), channel_id=1, replica_groups=mesh['dp'=16,'expert'=8] {'expert'}, dimensions={0} | all-to-all | bytes 3145728 | tf_op jit(solution)/shard_map/all_to_all | solution.py:198
  55.3 1.7 copy.99
  57.1 1.3 fusion.94
  59.0 6.1 stack.11
  65.1 6.8 all-to-all-start.2
  72.5 218.9 %all-to-all-done.2 = bf16[16,48,8192]{2,1,0:T(8,128)(2,1)} async-done(((bf16[16,48,8192]{2,1,0:T(8,128)(2,1)}), bf16[16,48,8192]{2,1,0:T(8,128)(2,1)}, u32[]{:S(2)}, u32[]{:S(2)}) %all-to-all-start.2) | async-done | bytes 12582944 | tf_op jit(solution)/shard_map/all_to_all | solution.py:209
  291.3 6.2 stack.9
  297.5 12.4 %all-to-all-start.1 = ((bf16[16,48,8192]{2,1,0:T(8,128)(2,1)}), bf16[16,48,8192]{2,1,0:T(8,128)(2,1)}, u32[]{:S(2)}, u32[]{:S(2)}) async-start(bf16[16,48,8192]{2,1,0:T(8,128)(2,1)} %stack.9), calls=%async_computation.1 | async-start | bytes 25165824 | tf_op jit(solution)/shard_map/all_to_all | solution.py:209
  310.2 4.5 convolution_convert_fusion.7
  314.7 4.5 convolution_convert_fusion.6
  319.3 198.0 %all-to-all-done.1 = bf16[16,48,8192]{2,1,0:T(8,128)(2,1)} async-done(((bf16[16,48,8192]{2,1,0:T(8,128)(2,1)}), bf16[16,48,8192]{2,1,0:T(8,128)(2,1)}, u32[]{:S(2)}, u32[]{:S(2)}) %all-to-all-start.1) | async-done | bytes 12582944 | tf_op jit(solution)/shard_map/all_to_all | solution.py:209
  517.3 4.5 convolution_convert_fusion.10
  521.8 4.5 convolution_convert_fusion.9
  526.3 4.5 convolution_convert_fusion.8
  530.9 4.7 convolution_convert_fusion.11
  535.5 5.8 fusion.5
  541.4 6.5 fusion.9
  547.9 5.8 fusion.19
  553.7 6.0 fusion.21
  559.7 5.8 fusion.13
  565.6 5.8 fusion.17
  572.4 1.9 multiply_convert_fusion.5
  574.6 6.4 fusion.15
  581.1 6.4 fusion.7
  589.6 6.4 fusion.11
  596.2 6.4 fusion.3
  604.6 9.2 %add_convert_fusion.1 = bf16[768,4096]{1,0:T(8,128)(2,1)S(1)} fusion(f32[768,4096]{1,0:T(8,128)} %fusion.7, f32[768,4096]{1,0:T(8,128)} %fusion.15, bf16[16,4096]{1,0:T(8,128)(2,1)S(1)} %bitcast.194, bf16[16,4096]{1,0:T(8,128)(2,1)S(1)} %bitcast.196, bf16[768,16]{0,1:T(8,128)(2,1)S(1)} %convolution_convert_fusion.4, bf16[768,16]{0,1:T(8,128)(2,1)} %copy-done.10), kind=kOutput, calls=%fused_computation.10 | convolution fusion | flops 214532096 | bytes 31768576 | tf_op jit(solution)/shard_map/dot_general | solution.py:12
  613.9 12.0 %add_convert_fusion = bf16[768,4096]{1,0:T(8,128)(2,1)} fusion(f32[768,4096]{1,0:T(8,128)} %fusion.3, f32[768,4096]{1,0:T(8,128)} %fusion.11, bf16[16,4096]{1,0:T(8,128)(2,1)S(1)} %bitcast.195, bf16[16,4096]{1,0:T(8,128)(2,1)S(1)} %bitcast.197, bf16[768,16]{0,1:T(8,128)(2,1)S(1)} %copy-done.12, bf16[768,16]{0,1:T(8,128)(2,1)S(1)} %copy-done.14), kind=kOutput, calls=%fused_computation.9 | convolution fusion | flops 214532096 | bytes 31768576 | tf_op jit(solution)/shard_map/dot_general | solution.py:12
  625.9 10.6 %pad_maximum_fusion = bf16[16,96,4224]{2,1,0:T(8,128)(2,1)} fusion(bf16[16,96,128]{2,1,0:T(8,128)(2,1)S(1)} %fusion.46, bf16[16,48,4096]{2,1,0:T(8,128)(2,1)} %bitcast.178, bf16[16,48,4096]{2,1,0:T(8,128)(2,1)S(1)} %bitcast.174), kind=kLoop, calls=%fused_computation.6 | loop fusion | flops 38928384 | bytes 25952256 | tf_op jit(solution)/shard_map/concatenate | solution.py:225
  637.2 1.4 fusion.97
  638.6 2.1 fusion.39
  643.2 5.6 fusion.93
  648.7 5.6 fusion.92
  654.3 8.7 %pad_maximum_fusion.2 = bf16[16,96,4096]{2,1,0:T(8,128)(2,1)} fusion(bf16[16,48,4096]{2,1,0:T(8,128)(2,1)S(1)} %bitcast.176, bf16[16,48,4096]{2,1,0:T(8,128)(2,1)S(1)} %bitcast.179), kind=kLoop, calls=%fused_computation.8 | loop fusion | flops 25165824 | bytes 25165824 | tf_op jit(solution)/shard_map/concatenate | solution.py:232
  663.1 8.6 %pad_maximum_fusion.1 = bf16[16,96,4096]{2,1,0:T(8,128)(2,1)} fusion(bf16[16,48,4096]{2,1,0:T(8,128)(2,1)S(1)} %bitcast.175, bf16[16,48,4096]{2,1,0:T(8,128)(2,1)S(1)} %bitcast.177), kind=kLoop, calls=%fused_computation.7 | loop fusion | flops 25165824 | bytes 25165824 | tf_op jit(solution)/shard_map/concatenate | solution.py:231
  671.6 72.0 %reduce-scatter.4.cloned.1.call-done = bf16[1,96,4224]{2,1,0:T(8,128)(2,1)} async-done(((bf16[16,96,4224]{2,1,0:T(8,128)(2,1)}), bf16[1,96,4224]{2,1,0:T(8,128)(2,1)}) %reduce-scatter.4.cloned.1.call-update) | async-done | bytes 811024
  745.6 16.5 %all-gather = bf16[16,96,48]{1,2,0:T(8,128)(2,1)S(1)} all-gather(bf16[1,96,48]{1,2,0:T(8,128)(2,1)S(1)} %copy.88), channel_id=1, replica_groups=mesh['dp'=16,'expert'=8] {'dp'}, dimensions={0}, use_global_device_ids=true | all-gather | bytes 156672 | tf_op jit(solution)/shard_map/all_gather | solution.py:229
  762.4 7.2 fusion.1
  770.7 2.4 fusion.2
  774.2 11.4 %all-to-all-start.3 = ((bf16[96,8,512]{2,0,1:T(8,128)(2,1)}), bf16[96,8,512]{2,0,1:T(8,128)(2,1)S(1)}, u32[]{:S(2)}, u32[]{:S(2)}) async-start(bf16[96,8,512]{2,0,1:T(8,128)(2,1)} %bitcast.168), calls=%async_computation.3 | async-start | bytes 1572864 | tf_op jit(solution)/shard_map/all_to_all | solution.py:239
  785.5 7.1 fusion
  792.6 5.2 all-to-all-done.3
  799.6 1.3 reduce_sum.29
  (121 shorter events, 23.7 us)
Async XLA Ops:
  7.2 519.2 %copy-start = (bf16[1,4096,16]{1,2,0:T(8,128)(2,1)S(1)}, bf16[1,4096,16]{1,2,0:T(8,128)(2,1)}, u32[]{:S(2)}) copy-start(bf16[1,4096,16]{1,2,0:T(8,128)(2,1)} %param.25) | copy-start | bytes 393220
  65.1 226.3 %all-to-all-start.2 = ((bf16[16,48,8192]{2,1,0:T(8,128)(2,1)}), bf16[16,48,8192]{2,1,0:T(8,128)(2,1)}, u32[]{:S(2)}, u32[]{:S(2)}) async-start(bf16[16,48,8192]{2,1,0:T(8,128)(2,1)} %stack.11), calls=%async_computation.2 | async-start | bytes 25165824 | tf_op jit(solution)/shard_map/all_to_all | solution.py:209
  297.5 12.7 %copy-start.6 = (bf16[1,16,4096]{2,1,0:T(8,128)(2,1)S(1)}, bf16[1,16,4096]{2,1,0:T(8,128)(2,1)}, u32[]{:S(2)}) copy-start(bf16[1,16,4096]{2,1,0:T(8,128)(2,1)} %param.22) | copy-start | bytes 393220
  297.5 219.8 %all-to-all-start.1 = ((bf16[16,48,8192]{2,1,0:T(8,128)(2,1)}), bf16[16,48,8192]{2,1,0:T(8,128)(2,1)}, u32[]{:S(2)}, u32[]{:S(2)}) async-start(bf16[16,48,8192]{2,1,0:T(8,128)(2,1)} %stack.9), calls=%async_computation.1 | async-start | bytes 25165824 | tf_op jit(solution)/shard_map/all_to_all | solution.py:209
  309.9 4.8 copy-start.7
  309.9 433.7 %reduce-scatter.4.cloned.1.call-start = ((), (), s32[]{:S(2)}) async-start(), calls=%async_computation.5 | async-start | bytes 13787136
  314.7 273.2 %copy-start.15 = (bf16[768,16]{0,1:T(8,128)(2,1)}, bf16[768,16]{0,1:T(8,128)(2,1)S(1)}, u32[]{:S(2)}) copy-start(bf16[768,16]{0,1:T(8,128)(2,1)S(1)} %convolution_convert_fusion.7) | copy-start | bytes 73732
  319.3 269.1 %copy-start.24 = (bf16[768,16]{0,1:T(8,128)(2,1)}, bf16[768,16]{0,1:T(8,128)(2,1)S(1)}, u32[]{:S(2)}) copy-start(bf16[768,16]{0,1:T(8,128)(2,1)S(1)} %convolution_convert_fusion.6) | copy-start | bytes 73732
  521.8 50.1 %copy-start.17 = (bf16[768,16]{0,1:T(8,128)(2,1)}, bf16[768,16]{0,1:T(8,128)(2,1)S(1)}, u32[]{:S(2)}) copy-start(bf16[768,16]{0,1:T(8,128)(2,1)S(1)} %convolution_convert_fusion.10) | copy-start | bytes 73732
  526.3 46.1 %copy-start.26 = (bf16[768,16]{0,1:T(8,128)(2,1)}, bf16[768,16]{0,1:T(8,128)(2,1)S(1)}, u32[]{:S(2)}) copy-start(bf16[768,16]{0,1:T(8,128)(2,1)S(1)} %convolution_convert_fusion.9) | copy-start | bytes 73732
  530.9 56.7 %copy-start.19 = (bf16[768,16]{0,1:T(8,128)(2,1)}, bf16[768,16]{0,1:T(8,128)(2,1)S(1)}, u32[]{:S(2)}) copy-start(bf16[768,16]{0,1:T(8,128)(2,1)S(1)} %convolution_convert_fusion.8) | copy-start | bytes 73732
  530.9 4.7 copy-start.4
  535.5 35.9 %copy-start.21 = (bf16[768,16]{0,1:T(8,128)(2,1)}, bf16[768,16]{0,1:T(8,128)(2,1)S(1)}, u32[]{:S(2)}) copy-start(bf16[768,16]{0,1:T(8,128)(2,1)S(1)} %convolution_convert_fusion.11) | copy-start | bytes 73732
  541.4 6.5 copy-start.28
  553.7 6.0 copy-start.3
  565.5 5.9 copy-start.9
  565.5 6.3 copy-start.8
  565.6 6.9 copy-start.23
  581.1 23.1 %copy-start.10 = (bf16[768,16]{0,1:T(8,128)(2,1)}, bf16[768,16]{0,1:T(8,128)(2,1)S(1)}, u32[]{:S(2)}) copy-start(bf16[768,16]{0,1:T(8,128)(2,1)S(1)} %convolution_convert_fusion.5) | copy-start | bytes 73732
  589.4 13.2 %copy-start.5 = (bf16[448,768]{1,0:T(8,128)(2,1)}, bf16[448,768]{1,0:T(8,128)(2,1)S(1)}, u32[]{:S(2)}) copy-start(bf16[448,768]{1,0:T(8,128)(2,1)S(1)} %get-tuple-element.15) | copy-start | bytes 2064388
  589.6 13.2 %copy-start.11 = (bf16[768,16]{0,1:T(8,128)(2,1)}, bf16[768,16]{0,1:T(8,128)(2,1)S(1)}, u32[]{:S(2)}) copy-start(bf16[768,16]{0,1:T(8,128)(2,1)S(1)} %convolution_convert_fusion.2) | copy-start | bytes 73732
  596.2 6.6 copy-start.13
  604.6 9.3 %copy-start.12 = (bf16[768,16]{0,1:T(8,128)(2,1)S(1)}, bf16[768,16]{0,1:T(8,128)(2,1)}, u32[]{:S(2)}) copy-start(bf16[768,16]{0,1:T(8,128)(2,1)} %copy-done.11) | copy-start | bytes 73732
  604.6 9.3 %copy-start.14 = (bf16[768,16]{0,1:T(8,128)(2,1)S(1)}, bf16[768,16]{0,1:T(8,128)(2,1)}, u32[]{:S(2)}) copy-start(bf16[768,16]{0,1:T(8,128)(2,1)} %copy-done.13) | copy-start | bytes 73732
  636.5 0.7 copy-start.22
  636.5 2.1 copy-start.20
  636.5 4.2 copy-start.27
  636.5 4.4 copy-start.25
  636.5 5.4 copy-start.18
  636.5 5.7 copy-start.16
  762.4 8.3 %copy-start.2 = (bf16[16,96,4096]{2,1,0:T(8,128)(2,1)S(1)}, bf16[16,96,4096]{2,1,0:T(8,128)(2,1)}, u32[]{:S(2)}) copy-start(bf16[16,96,4096]{2,1,0:T(8,128)(2,1)} %pad_maximum_fusion.1) | copy-start | bytes 37748740
  774.2 23.7 %all-to-all-start.3 = ((bf16[96,8,512]{2,0,1:T(8,128)(2,1)}), bf16[96,8,512]{2,0,1:T(8,128)(2,1)S(1)}, u32[]{:S(2)}, u32[]{:S(2)}) async-start(bf16[96,8,512]{2,0,1:T(8,128)(2,1)} %bitcast.168), calls=%async_computation.3 | async-start | bytes 1572864 | tf_op jit(solution)/shard_map/all_to_all | solution.py:239
  785.5 15.4 %copy-start.1 = (bf16[1,4096,16]{1,2,0:T(8,128)(2,1)S(1)}, bf16[1,4096,16]{1,2,0:T(8,128)(2,1)}, u32[]{:S(2)}) copy-start(bf16[1,4096,16]{1,2,0:T(8,128)(2,1)} %param.25) | copy-start | bytes 393220
Sparse Core Ops, SparseCore 0:
  636.7 106.9 reduce-scatter.3
